TPU v7x, 32 devices: a whole 2x2x4 slice. The times are simulated.
32 devices in a mesh: grp: 2 (over y), tile: 4 (over x, core), tp: 4 (over z).
Axes of the slice: x: 2, y: 2, z: 4, core: 2. Of those that a mesh axis runs over, the one named last changes fastest.
Arguments:
- atmos_state: bfloat16 [4096, 1536], P(('grp', 'tile')), may hold values from -6 to 6
- atmos_gain: float32 [1536], replicated, may hold values from 0.25 to 1.75
- w_first: bfloat16 [1536, 3072], P(('grp', 'tile'), 'tp'), may hold values from -0.15625 to 0.15625
- w_second: bfloat16 [1536, 3072], P(('grp', 'tile'), 'tp'), may hold values from -0.109375 to 0.109375
- flux_proj: bfloat16 [1536, 256], replicated, may hold values from -0.15625 to 0.15625
- remap_index: int32 [64, 3], P(('grp', 'tile', 'tp')), may hold values from 0 to 3
- remap_weight: bfloat16 [64, 3, 128, 128], P(('grp', 'tile', 'tp')), may hold values from -0.3125 to 0.3125
- ocean_state: bfloat16 [64, 128, 256], P(('grp', 'tile'), 'tp'), may hold values from -6 to 6
- depth_levels: int32 [64, 128], P(('grp', 'tile'), 'tp'), may hold values from 0 to 16
- conv_kernel: float32 [3, 3, 256], replicated, may hold values from -2 to 2
- ocean_gain: float32 [256], replicated, may hold values from 0.25 to 1.75
- ocean_w_in: bfloat16 [256, 1024], replicated, may hold values from -0.375 to 0.375
- ocean_w_out: bfloat16 [1024, 256], replicated, may hold values from -0.1875 to 0.1875
- ocean_cotangent: bfloat16 [64, 128, 256], P(('grp', 'tile'), 'tp'), may hold values from -6 to 6
Outputs:
- atmos_out: bfloat16 [4096, 1536], P(('grp', 'tile', 'tp'))
- ocean_out: bfloat16 [64, 128, 256], P(('grp', 'tile'), 'tp')
- weight_grads: float32 [2048, 256], P(('grp', 'tile', 'tp'))
Inputs may be any that keep to these rules, and one draw needn't show every extreme that they name: `remap_index`: index the 128-token blocks among the 512 atmosphere tokens of the same grp and tile indices as the ocean tile of that block. `depth_levels`: 0 marks land.
All inputs are finite; a program needn't handle non-finite values.
Results may differ from a plain program's by a relative error of at most 0.018.
Values may be sent and summed in bfloat16 or wider, within the bound.
No kernel may reach another device: no remote copies, remote signals or barrier semaphores. Data moves between devices by JAX's collectives and lax.ppermute only.
A program may use at most 64 MiB of HBM per device.

v0:
```python
import jax
import jax.numpy as jnp
from jax import lax
from jax.sharding import PartitionSpec as P

LEV = 16
epsilon = 1e-06


def with_halo(block, sides, width):
    for axis, dim in sides:
        count = lax.axis_size(axis)
        forward = [(i, i + 1) for i in range(count - 1)]
        backward = [(target, source) for source, target in forward]
        low = lax.ppermute(
            lax.slice_in_dim(block, block.shape[dim] - width, None, axis=dim), axis, forward
        )
        high = lax.ppermute(lax.slice_in_dim(block, 0, width, axis=dim), axis, backward)
        block = jnp.concatenate([low, block, high], axis=dim)
    return block


def rms_norm(values, gain):
    wide = values.astype(jnp.float32)
    scale = lax.rsqrt(jnp.mean(wide * wide, axis=-1, keepdims=True) + epsilon)
    return (wide * scale * gain).astype(jnp.bfloat16)


def on_device(
    atmos_state,
    atmos_gain,
    w_first,
    w_second,
    flux_proj,
    remap_index,
    remap_weight,
    ocean_state,
    depth_levels,
    conv_kernel,
    ocean_gain,
    ocean_w_in,
    ocean_w_out,
    ocean_cotangent,
):
    normed = rms_norm(atmos_state, atmos_gain)
    rows_all = atmos_state.shape[0]
    hsum = jnp.dot(
        normed,
        lax.all_gather(w_first, ("grp", "tile"), axis=0, tiled=True),
        preferred_element_type=jnp.float32,
    )
    hidden = jax.nn.gelu(hsum).astype(jnp.bfloat16)
    partial_sum = lax.dot_general(
        hidden,
        lax.all_gather(w_second, ("grp", "tile"), axis=0, tiled=True),
        (((1,), (1,)), ((), ())),
        preferred_element_type=jnp.float32,
    )
    rows_own = rows_all // lax.axis_size("tp")
    block_rows = remap_weight.shape[2]
    channels = flux_proj.shape[1]
    summed = lax.psum_scatter(
        partial_sum.astype(jnp.bfloat16), "tp", scatter_dimension=0, tiled=True
    ).astype(jnp.float32)
    own_rows = lax.dynamic_slice_in_dim(atmos_state, lax.axis_index("tp") * rows_own, rows_own, 0)
    atmos_out = (own_rows.astype(jnp.float32) + summed).astype(jnp.bfloat16)
    flux = jnp.dot(atmos_out, flux_proj, preferred_element_type=jnp.float32).astype(jnp.bfloat16)
    piece = lax.all_gather(flux, "tp", axis=0, tiled=True)
    count = piece.shape[0] // block_rows
    blocks = piece.reshape(count, block_rows, channels)
    targets = jnp.arange(count, dtype=jnp.int32)
    select = (remap_index[:, :, None] == targets[None, None, :]).astype(jnp.bfloat16)
    picked = jnp.einsum("bkj,jrc->bkrc", select, blocks, preferred_element_type=jnp.float32).astype(
        jnp.bfloat16
    )
    remapped = jnp.einsum(
        "bksr,bkrc->bsc", remap_weight, picked, preferred_element_type=jnp.float32
    )
    tile_x, tile_y, _ = ocean_state.shape
    levels = jnp.arange(channels, dtype=jnp.int32) // (channels // LEV)
    wet = (levels[None, None, :] < depth_levels[:, :, None]).astype(jnp.float32)
    moved = remapped.astype(jnp.bfloat16).reshape(tile_x, tile_y, channels)
    field = ((ocean_state.astype(jnp.float32) + moved.astype(jnp.float32)) * wet).astype(
        jnp.bfloat16
    )
    padded = with_halo(field, ((("grp", "tile"), 0), ("tp", 1)), 1).astype(jnp.float32)
    conv = jnp.zeros((tile_x, tile_y, channels), jnp.float32)
    for i in range(3):
        for j in range(3):
            conv = conv + conv_kernel[i, j] * padded[i : i + tile_x, j : j + tile_y]
    centred = conv - jnp.mean(conv, axis=-1, keepdims=True)
    variance = jnp.mean(centred * centred, axis=-1, keepdims=True)
    cells = tile_x * tile_y
    ocean_normed = (
        (centred * lax.rsqrt(variance + epsilon) * ocean_gain)
        .astype(jnp.bfloat16)
        .reshape(cells, channels)
    )
    flat_field = field.reshape(cells, channels)
    flat_wet = wet.reshape(cells, channels)
    pre = jnp.dot(ocean_normed, ocean_w_in, preferred_element_type=jnp.float32)
    activated, backward = jax.vjp(jax.nn.gelu, pre)
    activated = activated.astype(jnp.bfloat16)
    out = jnp.dot(activated, ocean_w_out, preferred_element_type=jnp.float32)
    ocean_out = (
        ((flat_field.astype(jnp.float32) + out) * flat_wet)
        .astype(jnp.bfloat16)
        .reshape(tile_x, tile_y, channels)
    )
    dout = (ocean_cotangent.reshape(cells, channels).astype(jnp.float32) * flat_wet).astype(
        jnp.bfloat16
    )
    dact = lax.dot_general(
        dout, ocean_w_out, (((1,), (1,)), ((), ())), preferred_element_type=jnp.float32
    )
    dpre = backward(dact)[0].astype(jnp.bfloat16)
    grad_in = lax.dot_general(
        dpre, ocean_normed, (((0,), (0,)), ((), ())), preferred_element_type=jnp.float32
    )
    grad_out = lax.dot_general(
        activated, dout, (((0,), (0,)), ((), ())), preferred_element_type=jnp.float32
    )
    terms = jnp.concatenate([grad_in, grad_out], axis=0)
    weight_grads = lax.psum_scatter(terms, ("grp", "tile", "tp"), scatter_dimension=0, tiled=True)
    return (atmos_out, ocean_out, weight_grads)


def solution(mesh):
    in_specs = (
        P(("grp", "tile"), None),
        P(),
        P(("grp", "tile"), "tp"),
        P(("grp", "tile"), "tp"),
        P(),
        P(("grp", "tile", "tp"), None),
        P(("grp", "tile", "tp"), None, None, None),
        P(("grp", "tile"), "tp", None),
        P(("grp", "tile"), "tp"),
        P(),
        P(),
        P(),
        P(),
        P(("grp", "tile"), "tp", None),
    )
    out_specs = (
        P(("grp", "tile", "tp"), None),
        P(("grp", "tile"), "tp", None),
        P(("grp", "tile", "tp"), None),
    )
    return jax.shard_map(
        on_device, mesh=mesh, in_specs=in_specs, out_specs=out_specs, check_vma=False
    )
```

profile of v0, /device:TPU:0, one launch (start us, length us, event | category | flops | bytes accessed | tf_op | source)
XLA Modules:
  0.0 300.5 jit_solution(9202283299108384426)
XLA Ops:
  7.2 0.0 copy-start
  7.2 0.0 all-gather.5.cloned.1.call-start
  7.2 0.7 all-gather.5.cloned.1.call-update
  7.9 0.0 all-gather.3.cloned.1.call-start
  8.0 0.7 all-gather.3.cloned.1.call-update
  8.7 0.0 reduce-scatter.3.cloned.1.call-start
  8.7 1.8 fusion
  10.5 31.0 %all-gather.5.cloned.1.call-done = bf16[1536,768]{1,0:T(8,128)(2,1)} async-done(((bf16[192,768]{1,0:T(8,128)(2,1)}), bf16[1536,768]{1,0:T(8,128)(2,1)}) %all-gather.5.cloned.1.call-update) | async-done | bytes 2359312 | tf_op jit(solution)/shard_map/all_gather | solution.py:55
  41.5 30.8 %all-gather.3.cloned.1.call-done = bf16[1536,768]{1,0:T(8,128)(2,1)} async-done(((bf16[192,768]{1,0:T(8,128)(2,1)}), bf16[1536,768]{1,0:T(8,128)(2,1)}) %all-gather.3.cloned.1.call-update) | async-done | bytes 2359312 | tf_op jit(solution)/shard_map/all_gather | solution.py:49
  72.3 6.9 %convolution_convert_fusion = bf16[512,1536]{1,0:T(8,128)(2,1)} fusion(bf16[1536,768]{1,0:T(8,128)(2,1)} %all-gather.5.cloned.1.call-done, bf16[1536,768]{1,0:T(8,128)(2,1)} %all-gather.3.cloned.1.call-done, bf16[512,1536]{1,0:T(8,128)(2,1)S(1)} %copy-done.1, f32[1536]{0:T(1024)S(1)} %copy-done.12, f32[512]{0:T(512)S(1)} %add_rsqrt_fusion.1), kind=kOutput, calls=%fused_computation.5 | convolution fusion | flops 2423390208 | bytes 7872512 | tf_op jit(solution)/shard_map/dot_general | solution.py:53
  79.2 0.0 reduce-scatter.3.cloned.1.call-update
  79.2 0.0 copy-start.9
  79.2 0.0 reduce-scatter.5.cloned.1.call-start
  79.3 0.6 copy-done.7
  79.9 0.1 lt.27
  80.0 34.8 %reduce-scatter.3.cloned.1.call-done = bf16[128,1536]{1,0:T(8,128)(2,1)} async-done(((bf16[512,1536]{1,0:T(8,128)(2,1)}), bf16[128,1536]{1,0:T(8,128)(2,1)}) %reduce-scatter.3.cloned.1.call-update) | async-done | bytes 393232 | tf_op jit(solution)/shard_map/reduce_scatter | solution.py:62
  114.8 1.1 add_convert_fusion
  115.9 0.0 copy-start.2
  115.9 0.0 copy-start.6
  116.0 0.3 convolution_convert_fusion.1
  116.2 0.0 copy-start.5
  116.3 0.0 copy-start.8
  116.3 14.6 %all_gather.11 = bf16[512,256]{1,0:T(8,128)(2,1)S(1)} all-gather(bf16[128,256]{1,0:T(8,128)(2,1)S(1)} %convolution_convert_fusion.1), channel_id=1, replica_groups=mesh['grp'=2,'tile'=4,'tp'=4] {'tp'}, dimensions={0}, use_global_device_ids=true | all-gather | bytes 327680 | tf_op jit(solution)/shard_map/all_gather | solution.py:68
  130.8 0.4 fusion.41
  131.2 0.2 fusion.19
  131.5 0.1 select_convert_fusion
  131.6 1.3 collective-permute-start.1
  132.9 3.0 %collective-permute-start = (bf16[1,32,256]{2,1,0:T(8,128)(2,1)S(1)}, bf16[1,32,256]{2,1,0:T(8,128)(2,1)S(1)}, u32[]{:S(2)}, u32[]{:S(2)}) collective-permute-start(bf16[1,32,256]{2,1,0:T(8,128)(2,1)S(1)} %get-tuple-element.7), channel_id=1, source_target_pairs={{0,4},{4,8},{8,12},{12,16},{16,20},{20,24},{24,28},{1,5},{5,9},{9,... | collective-permute-start | bytes 49160 | tf_op jit(solution)/shard_map/ppermute | solution.py:15
  136.0 0.1 fusion.32
  136.1 0.7 collective-permute-done
  136.8 1.3 collective-permute-start.3
  138.1 4.5 %collective-permute-start.2 = (bf16[10,1,256]{2,1,0:T(2,128)(2,1)S(1)}, bf16[10,1,256]{2,1,0:T(2,128)(2,1)S(1)}, u32[]{:S(2)}, u32[]{:S(2)}) collective-permute-start(bf16[10,1,256]{2,1,0:T(2,128)(2,1)S(1)} %get-tuple-element.5), channel_id=1, source_target_pairs={{0,1},{1,2},{2,3},{4,5},{5,6},{6,7},{8,9},{9,10},{10,11},{12,13},{... | collective-permute-start | bytes 15368 | tf_op jit(solution)/shard_map/ppermute | solution.py:15
  142.7 1.3 collective-permute-done.2
  144.0 0.1 maximum_convert_fusion
  144.1 0.0 copy-start.3
  144.1 0.3 fusion.57
  144.4 0.2 multiply_reduce_fusion
  144.6 0.2 copy-done.10
  144.8 0.1 multiply_convert_fusion.1
  144.9 0.2 copy-done.3
  145.1 0.3 fusion.63
  145.4 0.6 fusion.56
  146.0 3.1 %fusion.30 = f32[1024,256]{1,0:T(8,128)} fusion(bf16[256,256]{1,0:T(8,128)(2,1)S(1)} %bitcast.50, f32[256,1024]{1,0:T(8,128)S(1)} %fusion.63, bf16[256,256]{1,0:T(8,128)(2,1)S(1)} %fusion.32, bf16[1024,256]{1,0:T(8,128)(2,1)} %param.26), kind=kOutput, calls=%fused_computation.38 | convolution fusion | flops 273678336 | bytes 2883584 | tf_op jit(solution)/shard_map/dot_general | solution.py:117
  149.2 2.7 pad_maximum_fusion
  151.9 0.0 reduce-scatter.5.cloned.1.call-update
  151.9 1.0 copy-done.11
  152.9 1.1 fusion.20
  154.0 139.9 %reduce-scatter.5.cloned.1.call-done = f32[64,256]{1,0:T(8,128)} async-done(((f32[2048,256]{1,0:T(8,128)}), f32[64,256]{1,0:T(8,128)}) %reduce-scatter.5.cloned.1.call-update) | async-done | bytes 65552 | tf_op jit(solution)/shard_map/reduce_scatter | solution.py:124
  (24 shorter events, 0.1 us)
Async XLA Ops:
  7.2 108.8 %copy-start = (bf16[1536,256]{1,0:T(8,128)(2,1)S(1)}, bf16[1536,256]{1,0:T(8,128)(2,1)}, u32[]{:S(2)}) copy-start(bf16[1536,256]{1,0:T(8,128)(2,1)} %param.18) | copy-start | bytes 2359300
  7.2 65.1 %copy-start.1 = (bf16[512,1536]{1,0:T(8,128)(2,1)S(1)}, bf16[512,1536]{1,0:T(8,128)(2,1)}, u32[]{:S(2)}) copy-start(bf16[512,1536]{1,0:T(8,128)(2,1)} %param.14) | copy-start | bytes 4718596
  7.2 65.1 %copy-start.12 = (f32[1536]{0:T(1024)S(1)}, f32[1536]{0:T(1024)}, u32[]{:S(2)}) copy-start(f32[1536]{0:T(1024)} %param.15) | copy-start | bytes 18436
  7.2 34.3 %all-gather.5.cloned.1.call-start = ((), (), s32[]{:S(2)}) async-start(), calls=%async_computation.3 | async-start | bytes 2654208 | tf_op jit(solution)/shard_map/all_gather | solution.py:55
  7.9 64.4 %all-gather.3.cloned.1.call-start = ((), (), s32[]{:S(2)}) async-start(), calls=%async_computation.2 | async-start | bytes 2654208 | tf_op jit(solution)/shard_map/all_gather | solution.py:49
  8.7 106.1 %reduce-scatter.3.cloned.1.call-start = ((), (), s32[]{:S(2)}) async-start(), calls=%async_computation.4 | async-start | bytes 1966080 | tf_op jit(solution)/shard_map/reduce_scatter | solution.py:62
  79.2 0.7 copy-start.7
  79.2 51.6 %copy-start.9 = (s32[2,3]{1,0:T(2,128)S(1)}, s32[2,3]{1,0:T(2,128)}, u32[]{:S(2)}) copy-start(s32[2,3]{1,0:T(2,128)} %param.19) | copy-start | bytes 76
  79.2 214.7 %reduce-scatter.5.cloned.1.call-start = ((), (), s32[]{:S(2)}) async-start(), calls=%async_computation.5 | async-start | bytes 2162688 | tf_op jit(solution)/shard_map/reduce_scatter | solution.py:124
  80.0 51.2 %copy-start.4 = (bf16[2,3,128,128]{3,2,1,0:T(8,128)(2,1)S(1)}, bf16[2,3,128,128]{3,2,1,0:T(8,128)(2,1)}, u32[]{:S(2)}) copy-start(bf16[2,3,128,128]{3,2,1,0:T(8,128)(2,1)} %param.20) | copy-start | bytes 589828
  115.9 15.5 %copy-start.2 = (bf16[128,1536]{1,0:T(8,128)(2,1)}, bf16[128,1536]{1,0:T(8,128)(2,1)S(1)}, u32[]{:S(2)}) copy-start(bf16[128,1536]{1,0:T(8,128)(2,1)S(1)} %add_convert_fusion) | copy-start | bytes 1179652
  115.9 15.5 %copy-start.6 = (bf16[8,32,256]{2,1,0:T(8,128)(2,1)S(1)}, bf16[8,32,256]{2,1,0:T(8,128)(2,1)}, u32[]{:S(2)}) copy-start(bf16[8,32,256]{2,1,0:T(8,128)(2,1)} %param.21) | copy-start | bytes 393220
  116.2 19.7 %copy-start.5 = (bf16[8,32,256]{2,1,0:T(8,128)(2,1)S(1)}, bf16[8,32,256]{2,1,0:T(8,128)(2,1)}, u32[]{:S(2)}) copy-start(bf16[8,32,256]{2,1,0:T(8,128)(2,1)} %param.27) | copy-start | bytes 393220
  116.3 26.4 %copy-start.8 = (f32[3,3,256]{2,1,0:T(4,128)S(1)}, f32[3,3,256]{2,1,0:T(4,128)}, u32[]{:S(2)}) copy-start(f32[3,3,256]{2,1,0:T(4,128)} %param.23) | copy-start | bytes 27652
  131.6 4.5 %collective-permute-start.1 = (bf16[1,32,256]{2,1,0:T(8,128)(2,1)S(1)}, bf16[1,32,256]{2,1,0:T(8,128)(2,1)S(1)}, u32[]{:S(2)}, u32[]{:S(2)}) collective-permute-start(bf16[1,32,256]{2,1,0:T(8,128)(2,1)S(1)} %get-tuple-element.8), channel_id=1, source_target_pairs={{4,0},{8,4},{12,8},{16,12},{20,16},{24,20},{28,24},{5,1},{9,5},{13... | collective-permute-start | bytes 49160 | tf_op jit(solution)/shard_map/ppermute | solution.py:18
  132.9 3.9 %collective-permute-start = (bf16[1,32,256]{2,1,0:T(8,128)(2,1)S(1)}, bf16[1,32,256]{2,1,0:T(8,128)(2,1)S(1)}, u32[]{:S(2)}, u32[]{:S(2)}) collective-permute-start(bf16[1,32,256]{2,1,0:T(8,128)(2,1)S(1)} %get-tuple-element.7), channel_id=1, source_target_pairs={{0,4},{4,8},{8,12},{12,16},{16,20},{20,24},{24,28},{1,5},{5,9},{9,... | collective-permute-start | bytes 49160 | tf_op jit(solution)/shard_map/ppermute | solution.py:15
  136.8 5.9 %collective-permute-start.3 = (bf16[10,1,256]{2,1,0:T(2,128)(2,1)S(1)}, bf16[10,1,256]{2,1,0:T(2,128)(2,1)S(1)}, u32[]{:S(2)}, u32[]{:S(2)}) collective-permute-start(bf16[10,1,256]{2,1,0:T(2,128)(2,1)S(1)} %get-tuple-element.6), channel_id=1, source_target_pairs={{1,0},{2,1},{3,2},{5,4},{6,5},{7,6},{9,8},{10,9},{11,10},{13,12},{... | collective-permute-start | bytes 15368 | tf_op jit(solution)/shard_map/ppermute | solution.py:18
  138.1 5.9 %collective-permute-start.2 = (bf16[10,1,256]{2,1,0:T(2,128)(2,1)S(1)}, bf16[10,1,256]{2,1,0:T(2,128)(2,1)S(1)}, u32[]{:S(2)}, u32[]{:S(2)}) collective-permute-start(bf16[10,1,256]{2,1,0:T(2,128)(2,1)S(1)} %get-tuple-element.5), channel_id=1, source_target_pairs={{0,1},{1,2},{2,3},{4,5},{5,6},{6,7},{8,9},{9,10},{10,11},{12,13},{... | collective-permute-start | bytes 15368 | tf_op jit(solution)/shard_map/ppermute | solution.py:15
  144.1 0.7 copy-start.10
  144.1 1.0 copy-start.3
  151.9 1.0 copy-start.11
Sparse Core Ops, SparseCore 0:
  9.9 31.5 all-gather.4
  43.4 28.8 all-gather.2
  79.3 35.4 reduce-scatter.2
  152.0 141.8 reduce-scatter.4
where the time goes:
time: 301 us; the launch traced here: 300 us
  waiting for transfers between devices  240 us (80%)
  blocking collectives  14.6 us (5%)
  between operations  14 us (5%)
  matrix products  12.9 us (4%)
  starting transfers between devices  10.3 us (3%)
  other arithmetic  6.51 us (2%)
    reduce_scatter x1, waiting for transfers between devices, on_device(): lax.psum_scatter(terms, ('grp', 'tile', 'tp'), scatter_dimension=0, tiled...  140 us
    reduce_scatter x1, waiting for transfers between devices, on_device(): lax.psum_scatter(partial_sum.astype(jnp.bfloat16), 'tp', scatter_dimensio...  34.8 us
    all_gather x1, waiting for transfers between devices, on_device(): lax.all_gather(w_second, ('grp', 'tile'), axis=0, tiled=True)  31 us
    all_gather x1, waiting for transfers between devices, on_device(): lax.all_gather(w_first, ('grp', 'tile'), axis=0, tiled=True)  30.8 us
    all_gather x1, blocking collectives, on_device(): piece = lax.all_gather(flux, 'tp', axis=0, tiled=True)  14.6 us
    ppermute x2, starting transfers between devices, with_halo(): lax.ppermute(lax.slice_in_dim(block, block.shape[dim] - width, None, axis...  7.58 us
    dot_general x1, matrix products, on_device(): lax.dot_general(hidden, lax.all_gather(w_second, ('grp', 'tile'), axis=0,...  6.86 us
  transfers between devices with their start and end apart: 8, of which 6 were waited for; matrix products, arithmetic and copies ran while one was open for 1% of the time, Pallas kernels for 0%

commit v1 on v0

--- a/solution.py
+++ b/solution.py
@@ -5,6 +5,27 @@
 
 LEV = 16
 epsilon = 1e-06
+
+
+def gather_around(x, axis, dim):
+    peers, here, rows = (lax.axis_size(axis), lax.axis_index(axis), x.shape[dim])
+    forward = [(i, (i + 1) % peers) for i in range(peers)]
+    left = [(i, (i - 1) % peers) for i in range(peers)]
+    out = jnp.zeros((*x.shape[:dim], peers * rows, *x.shape[dim + 1 :]), x.dtype)
+    out = lax.dynamic_update_slice_in_dim(out, x, here * rows, axis=dim)
+    from_left = from_right = x
+    middle = peers // 2
+    for turn in range(1, middle + 1):
+        from_left = lax.ppermute(from_left, axis, forward)
+        out = lax.dynamic_update_slice_in_dim(
+            out, from_left, (here - turn) % peers * rows, axis=dim
+        )
+        if turn < peers - middle:
+            from_right = lax.ppermute(from_right, axis, left)
+            out = lax.dynamic_update_slice_in_dim(
+                out, from_right, (here + turn) % peers * rows, axis=dim
+            )
+    return out
 
 
 def with_halo(block, sides, width):
@@ -52,7 +73,7 @@
     hidden = jax.nn.gelu(hsum).astype(jnp.bfloat16)
     partial_sum = lax.dot_general(
         hidden,
-        lax.all_gather(w_second, ("grp", "tile"), axis=0, tiled=True),
+        gather_around(w_second, ("grp", "tile"), 0),
         (((1,), (1,)), ((), ())),
         preferred_element_type=jnp.float32,
     )

time: 301 us -> 283 us (0.940)
  waiting for transfers between devices: 240 us -> 199 us
  starting transfers between devices: 10.3 us -> 25.8 us
  local copies, waits for them, and re-layouts: 2.17 us -> 8.64 us
    all_gather x1 -> x0, waiting for transfers between devices: 31 us -> none  [on_device(): lax.all_gather(w_second, ('grp', 'tile'), axis=0, tiled=True)]
    all_gather x1, waiting for transfers between devices: 30.8 us -> 1.65 us  [on_device(): lax.all_gather(w_first, ('grp', 'tile'), axis=0, tiled=True)]
    ppermute x0 -> x7, starting transfers between devices: none -> 17.1 us  [the longest x4 9.26 us: gather_around(): from_left = lax.ppermute(from_left, axis, forward)]
    ppermute x0 -> x7, waiting for transfers between devices: none -> 12.8 us  [the longest x4 8.02 us: gather_around(): from_left = lax.ppermute(from_left, axis, forward)]
    dynamic_update_slice x0 -> x8, local copies, waits for them, and re-layouts: none -> 6.88 us  [the longest x4 3.95 us: gather_around(): lax.dynamic_update_slice_in_dim(out, from_left, (here - turn) % peers * r...]
    reduce_scatter x1, waiting for transfers between devices: 34.8 us -> 40.7 us  [on_device(): lax.psum_scatter(partial_sum.astype(jnp.bfloat16), 'tp', scatter_dimensio...]
    ppermute x2, waiting for transfers between devices: 0.01 us -> 3.36 us  [with_halo(): lax.ppermute(lax.slice_in_dim(block, 0, width, axis=dim), axis, backward)]
  transfers between devices with their start and end apart: 8 -> 14, of which waited for: 6 -> 10; matrix products, arithmetic and copies ran while one was open for 1% -> 4% of each run, Pallas kernels for 0% -> 0%
where the time goes in v1:
time: 283 us
  waiting for transfers between devices  199 us (70%)
  starting transfers between devices  25.8 us (9%)
  blocking collectives  14.4 us (5%)
  between operations  14 us (5%)
  matrix products  13.9 us (5%)
  local copies, waits for them, and re-layouts  8.64 us (3%)
  other arithmetic  6.47 us (2%)
    reduce_scatter x1, waiting for transfers between devices, on_device(): lax.psum_scatter(terms, ('grp', 'tile', 'tp'), scatter_dimension=0, tiled...  139 us
    reduce_scatter x1, waiting for transfers between devices, on_device(): lax.psum_scatter(partial_sum.astype(jnp.bfloat16), 'tp', scatter_dimensio...  40.7 us
    all_gather x1, blocking collectives, on_device(): piece = lax.all_gather(flux, 'tp', axis=0, tiled=True)  14.4 us
    ppermute x4, starting transfers between devices, gather_around(): from_left = lax.ppermute(from_left, axis, forward)  9.26 us
    ppermute x4, waiting for transfers between devices, gather_around(): from_left = lax.ppermute(from_left, axis, forward)  8.02 us
    ppermute x3, starting transfers between devices, gather_around(): from_right = lax.ppermute(from_right, axis, left)  7.88 us
    dot_general x1, matrix products, on_device(): lax.dot_general(hidden, gather_around(w_second, ('grp', 'tile'), 0), (((1...  6.83 us
    ppermute x2, starting transfers between devices, with_halo(): lax.ppermute(lax.slice_in_dim(block, block.shape[dim] - width, None, axis...  5.97 us
  transfers between devices with their start and end apart: 14, of which 10 were waited for; matrix products, arithmetic and copies ran while one was open for 4% of the time, Pallas kernels for 0%

profile of v1, /device:TPU:0, one launch (start us, length us, event | category | flops | bytes accessed | tf_op | source)
XLA Modules:
  0.0 282.7 jit_solution(12966024250056725887)
XLA Ops:
  7.2 0.7 all-gather.2.cloned.1.call-update
  8.0 0.5 collective-permute-start
  8.5 2.9 %collective-permute-start.1 = (bf16[192,768]{1,0:T(8,128)(2,1)}, bf16[192,768]{1,0:T(8,128)(2,1)S(1)}, u32[]{:S(2)}, u32[]{:S(2)}) collective-permute-start(bf16[192,768]{1,0:T(8,128)(2,1)} %param.17), channel_id=1, source_target_pairs={{0,28},{4,0},{8,4},{12,8},{16,12},{20,16},{24,20},{28,24},{1,29},{... | collective-permute-start | bytes 884744 | tf_op jit(solution)/shard_map/ppermute | solution.py:24
  11.4 1.8 fusion
  13.2 3.3 %collective-permute-done = bf16[192,768]{1,0:T(8,128)(2,1)S(1)} collective-permute-done((bf16[192,768]{1,0:T(8,128)(2,1)}, bf16[192,768]{1,0:T(8,128)(2,1)S(1)}, u32[]{:S(2)}, u32[]{:S(2)}) %collective-permute-start) | collective-permute-done | bytes 294944 | tf_op jit(solution)/shard_map/ppermute | solution.py:19
  16.6 0.6 collective-permute-start.2
  17.2 0.9 collective-permute-done.1
  18.1 2.7 collective-permute-start.3
  20.8 1.6 broadcast_in_dim.2
  22.4 0.7 constant_dynamic-update-slice_fusion.7
  23.2 1.7 collective-permute-done.2
  24.8 3.7 %collective-permute-start.4 = (bf16[192,768]{1,0:T(8,128)(2,1)}, bf16[192,768]{1,0:T(8,128)(2,1)S(1)}, u32[]{:S(2)}, u32[]{:S(2)}) collective-permute-start(bf16[192,768]{1,0:T(8,128)(2,1)} %collective-permute-done.2), channel_id=1, source_target_pairs={{0,4},{4,8},{8,12},{12,16},{16,20},{20,24},{24,28},{28,0},{1,5},{5... | collective-permute-start | bytes 884744 | tf_op jit(solution)/shard_map/ppermute | solution.py:19
  28.5 0.8 constant_dynamic-update-slice_fusion.6
  29.3 0.7 constant_dynamic-update-slice_fusion.5
  30.0 2.2 collective-permute-start.5
  32.3 1.7 constant_dynamic-update-slice_fusion.4
  34.0 4.4 %collective-permute-start.6 = (bf16[192,768]{1,0:T(8,128)(2,1)S(1)}, bf16[192,768]{1,0:T(8,128)(2,1)S(1)}, u32[]{:S(2)}, u32[]{:S(2)}) collective-permute-start(bf16[192,768]{1,0:T(8,128)(2,1)S(1)} %collective-permute-done.4), channel_id=1, source_target_pairs={{0,4},{4,8},{8,12},{12,16},{16,20},{20,24},{24,28},{28,0},{1,5},{5... | collective-permute-start | bytes 884744 | tf_op jit(solution)/shard_map/ppermute | solution.py:19
  38.4 0.7 constant_dynamic-update-slice_fusion.3
  39.1 0.7 constant_dynamic-update-slice_fusion.2
  39.8 3.9 %collective-permute-done.5 = bf16[192,768]{1,0:T(8,128)(2,1)S(1)} collective-permute-done((bf16[192,768]{1,0:T(8,128)(2,1)S(1)}, bf16[192,768]{1,0:T(8,128)(2,1)S(1)}, u32[]{:S(2)}, u32[]{:S(2)}) %collective-permute-start.5) | collective-permute-done | bytes 294944 | tf_op jit(solution)/shard_map/ppermute | solution.py:24
  43.7 0.7 constant_dynamic-update-slice_fusion.1
  44.4 3.0 %collective-permute-done.6 = bf16[192,768]{1,0:T(8,128)(2,1)S(1)} collective-permute-done((bf16[192,768]{1,0:T(8,128)(2,1)S(1)}, bf16[192,768]{1,0:T(8,128)(2,1)S(1)}, u32[]{:S(2)}, u32[]{:S(2)}) %collective-permute-start.6) | collective-permute-done | bytes 294944 | tf_op jit(solution)/shard_map/ppermute | solution.py:19
  47.5 0.8 constant_dynamic-update-slice_fusion
  48.2 1.7 all-gather.2.cloned.1.call-done
  49.9 6.8 %convolution_convert_fusion = bf16[512,1536]{1,0:T(8,128)(2,1)} fusion(bf16[1536,768]{1,0:T(8,128)(2,1)} %constant_dynamic-update-slice_fusion, bf16[1536,768]{1,0:T(8,128)(2,1)} %all-gather.2.cloned.1.call-done, bf16[512,1536]{1,0:T(8,128)(2,1)S(1)} %copy-done.1, f32[1536]{0:T(1024)S(1)} %copy-done.12, f32[512]{0:T(512)S(1)} %add_rsqrt_fusion.1), kind=kOutput, calls=%fused_computation.5 | convolution fusion | flops 2423390208 | bytes 7872512 | tf_op jit(solution)/shard_map/dot_general | solution.py:74
  56.9 40.7 %reduce-scatter.3.cloned.1.call-done = bf16[128,1536]{1,0:T(8,128)(2,1)} async-done(((bf16[512,1536]{1,0:T(8,128)(2,1)}), bf16[128,1536]{1,0:T(8,128)(2,1)}) %reduce-scatter.3.cloned.1.call-update) | async-done | bytes 393232 | tf_op jit(solution)/shard_map/reduce_scatter | solution.py:83
  97.7 1.1 add_convert_fusion
  98.8 0.3 convolution_convert_fusion.1
  99.1 14.4 %all_gather.7 = bf16[512,256]{1,0:T(8,128)(2,1)S(1)} all-gather(bf16[128,256]{1,0:T(8,128)(2,1)S(1)} %convolution_convert_fusion.1), channel_id=1, replica_groups=mesh['grp'=2,'tile'=4,'tp'=4] {'tp'}, dimensions={0}, use_global_device_ids=true | all-gather | bytes 327680 | tf_op jit(solution)/shard_map/all_gather | solution.py:89
  113.5 0.4 fusion.41
  113.9 0.2 fusion.19
  114.1 0.1 select_convert_fusion
  114.3 1.4 collective-permute-start.7
  115.7 1.3 collective-permute-start.8
  117.0 0.1 fusion.32
  117.1 3.4 %collective-permute-done.8 = bf16[1,32,256]{2,1,0:T(8,128)(2,1)S(1)} collective-permute-done((bf16[1,32,256]{2,1,0:T(8,128)(2,1)S(1)}, bf16[1,32,256]{2,1,0:T(8,128)(2,1)S(1)}, u32[]{:S(2)}, u32[]{:S(2)}) %collective-permute-start.8) | collective-permute-done | bytes 16416 | tf_op jit(solution)/shard_map/ppermute | solution.py:39
  120.5 1.3 collective-permute-start.10
  121.8 4.5 %collective-permute-start.9 = (bf16[10,1,256]{2,1,0:T(2,128)(2,1)S(1)}, bf16[10,1,256]{2,1,0:T(2,128)(2,1)S(1)}, u32[]{:S(2)}, u32[]{:S(2)}) collective-permute-start(bf16[10,1,256]{2,1,0:T(2,128)(2,1)S(1)} %get-tuple-element.5), channel_id=1, source_target_pairs={{0,1},{1,2},{2,3},{4,5},{5,6},{6,7},{8,9},{9,10},{10,11},{12,13},{... | collective-permute-start | bytes 15368 | tf_op jit(solution)/shard_map/ppermute | solution.py:36
  126.4 1.3 collective-permute-done.9
  127.8 0.3 fusion.57
  128.1 0.2 multiply_reduce_fusion
  128.3 0.1 multiply_convert_fusion.1
  128.5 0.3 fusion.63
  128.8 0.6 fusion.56
  129.4 3.1 %fusion.30 = f32[1024,256]{1,0:T(8,128)} fusion(bf16[256,256]{1,0:T(8,128)(2,1)S(1)} %bitcast.50, f32[256,1024]{1,0:T(8,128)S(1)} %fusion.63, bf16[256,256]{1,0:T(8,128)(2,1)S(1)} %fusion.32, bf16[1024,256]{1,0:T(8,128)(2,1)} %param.26), kind=kOutput, calls=%fused_computation.38 | convolution fusion | flops 273678336 | bytes 2883584 | tf_op jit(solution)/shard_map/dot_general | solution.py:138
  132.5 2.7 pad_maximum_fusion
  135.2 2.2 fusion.20
  137.4 138.8 %reduce-scatter.5.cloned.1.call-done = f32[64,256]{1,0:T(8,128)} async-done(((f32[2048,256]{1,0:T(8,128)}), f32[64,256]{1,0:T(8,128)}) %reduce-scatter.5.cloned.1.call-update) | async-done | bytes 65552 | tf_op jit(solution)/shard_map/reduce_scatter | solution.py:145
  (44 shorter events, 0.4 us)
Async XLA Ops:
  7.2 91.6 %copy-start = (bf16[1536,256]{1,0:T(8,128)(2,1)S(1)}, bf16[1536,256]{1,0:T(8,128)(2,1)}, u32[]{:S(2)}) copy-start(bf16[1536,256]{1,0:T(8,128)(2,1)} %param.18) | copy-start | bytes 2359300
  7.2 15.3 %copy-start.4 = (bf16[192,768]{1,0:T(8,128)(2,1)S(1)}, bf16[192,768]{1,0:T(8,128)(2,1)}, u32[]{:S(2)}) copy-start(bf16[192,768]{1,0:T(8,128)(2,1)} %param.17) | copy-start | bytes 884740
  7.2 42.7 %all-gather.2.cloned.1.call-start = ((), (), s32[]{:S(2)}) async-start(), calls=%async_computation.2 | async-start | bytes 2654208 | tf_op jit(solution)/shard_map/all_gather | solution.py:70
  7.9 89.7 %reduce-scatter.3.cloned.1.call-start = ((), (), s32[]{:S(2)}) async-start(), calls=%async_computation.3 | async-start | bytes 1966080 | tf_op jit(solution)/shard_map/reduce_scatter | solution.py:83
  8.0 8.6 %collective-permute-start = (bf16[192,768]{1,0:T(8,128)(2,1)}, bf16[192,768]{1,0:T(8,128)(2,1)S(1)}, u32[]{:S(2)}, u32[]{:S(2)}) collective-permute-start(bf16[192,768]{1,0:T(8,128)(2,1)} %param.17), channel_id=1, source_target_pairs={{0,4},{4,8},{8,12},{12,16},{16,20},{20,24},{24,28},{28,0},{1,5},{5... | collective-permute-start | bytes 884744 | tf_op jit(solution)/shard_map/ppermute | solution.py:19
  8.5 9.6 %collective-permute-start.1 = (bf16[192,768]{1,0:T(8,128)(2,1)}, bf16[192,768]{1,0:T(8,128)(2,1)S(1)}, u32[]{:S(2)}, u32[]{:S(2)}) collective-permute-start(bf16[192,768]{1,0:T(8,128)(2,1)} %param.17), channel_id=1, source_target_pairs={{0,28},{4,0},{8,4},{12,8},{16,12},{20,16},{24,20},{28,24},{1,29},{... | collective-permute-start | bytes 884744 | tf_op jit(solution)/shard_map/ppermute | solution.py:24
  16.6 8.3 %collective-permute-start.2 = (bf16[192,768]{1,0:T(8,128)(2,1)S(1)}, bf16[192,768]{1,0:T(8,128)(2,1)}, u32[]{:S(2)}, u32[]{:S(2)}) collective-permute-start(bf16[192,768]{1,0:T(8,128)(2,1)S(1)} %collective-permute-done), channel_id=1, source_target_pairs={{0,4},{4,8},{8,12},{12,16},{16,20},{20,24},{24,28},{28,0},{1,5},{5... | collective-permute-start | bytes 884744 | tf_op jit(solution)/shard_map/ppermute | solution.py:19
  18.1 11.9 %collective-permute-start.3 = (bf16[192,768]{1,0:T(8,128)(2,1)S(1)}, bf16[192,768]{1,0:T(8,128)(2,1)S(1)}, u32[]{:S(2)}, u32[]{:S(2)}) collective-permute-start(bf16[192,768]{1,0:T(8,128)(2,1)S(1)} %collective-permute-done.1), channel_id=1, source_target_pairs={{0,28},{4,0},{8,4},{12,8},{16,12},{20,16},{24,20},{28,24},{1,29},{... | collective-permute-start | bytes 884744 | tf_op jit(solution)/shard_map/ppermute | solution.py:24
  22.4 27.5 %copy-start.1 = (bf16[512,1536]{1,0:T(8,128)(2,1)S(1)}, bf16[512,1536]{1,0:T(8,128)(2,1)}, u32[]{:S(2)}) copy-start(bf16[512,1536]{1,0:T(8,128)(2,1)} %param.14) | copy-start | bytes 4718596
  22.4 27.5 %copy-start.12 = (f32[1536]{0:T(1024)S(1)}, f32[1536]{0:T(1024)}, u32[]{:S(2)}) copy-start(f32[1536]{0:T(1024)} %param.15) | copy-start | bytes 18436
  24.8 9.2 %collective-permute-start.4 = (bf16[192,768]{1,0:T(8,128)(2,1)}, bf16[192,768]{1,0:T(8,128)(2,1)S(1)}, u32[]{:S(2)}, u32[]{:S(2)}) collective-permute-start(bf16[192,768]{1,0:T(8,128)(2,1)} %collective-permute-done.2), channel_id=1, source_target_pairs={{0,4},{4,8},{8,12},{12,16},{16,20},{20,24},{24,28},{28,0},{1,5},{5... | collective-permute-start | bytes 884744 | tf_op jit(solution)/shard_map/ppermute | solution.py:19
  30.0 13.7 %collective-permute-start.5 = (bf16[192,768]{1,0:T(8,128)(2,1)S(1)}, bf16[192,768]{1,0:T(8,128)(2,1)S(1)}, u32[]{:S(2)}, u32[]{:S(2)}) collective-permute-start(bf16[192,768]{1,0:T(8,128)(2,1)S(1)} %collective-permute-done.3), channel_id=1, source_target_pairs={{0,28},{4,0},{8,4},{12,8},{16,12},{20,16},{24,20},{28,24},{1,29},{... | collective-permute-start | bytes 884744 | tf_op jit(solution)/shard_map/ppermute | solution.py:24
  34.0 13.5 %collective-permute-start.6 = (bf16[192,768]{1,0:T(8,128)(2,1)S(1)}, bf16[192,768]{1,0:T(8,128)(2,1)S(1)}, u32[]{:S(2)}, u32[]{:S(2)}) collective-permute-start(bf16[192,768]{1,0:T(8,128)(2,1)S(1)} %collective-permute-done.4), channel_id=1, source_target_pairs={{0,4},{4,8},{8,12},{12,16},{16,20},{20,24},{24,28},{28,0},{1,5},{5... | collective-permute-start | bytes 884744 | tf_op jit(solution)/shard_map/ppermute | solution.py:19
  48.2 8.6 %copy-start.8 = (s32[8,32]{1,0:T(8,128)S(1)}, s32[8,32]{1,0:T(8,128)}, u32[]{:S(2)}) copy-start(s32[8,32]{1,0:T(8,128)} %param.22) | copy-start | bytes 3076
  56.7 56.8 %copy-start.10 = (s32[2,3]{1,0:T(2,128)S(1)}, s32[2,3]{1,0:T(2,128)}, u32[]{:S(2)}) copy-start(s32[2,3]{1,0:T(2,128)} %param.19) | copy-start | bytes 76
  56.7 57.1 %copy-start.5 = (bf16[2,3,128,128]{3,2,1,0:T(8,128)(2,1)S(1)}, bf16[2,3,128,128]{3,2,1,0:T(8,128)(2,1)}, u32[]{:S(2)}) copy-start(bf16[2,3,128,128]{3,2,1,0:T(8,128)(2,1)} %param.20) | copy-start | bytes 589828
  56.8 57.4 %copy-start.7 = (bf16[8,32,256]{2,1,0:T(8,128)(2,1)S(1)}, bf16[8,32,256]{2,1,0:T(8,128)(2,1)}, u32[]{:S(2)}) copy-start(bf16[8,32,256]{2,1,0:T(8,128)(2,1)} %param.21) | copy-start | bytes 393220
  56.8 219.4 %reduce-scatter.5.cloned.1.call-start = ((), (), s32[]{:S(2)}) async-start(), calls=%async_computation.4 | async-start | bytes 2162688 | tf_op jit(solution)/shard_map/reduce_scatter | solution.py:145
  56.9 60.1 %copy-start.6 = (bf16[8,32,256]{2,1,0:T(8,128)(2,1)S(1)}, bf16[8,32,256]{2,1,0:T(8,128)(2,1)}, u32[]{:S(2)}) copy-start(bf16[8,32,256]{2,1,0:T(8,128)(2,1)} %param.27) | copy-start | bytes 393220
  98.8 29.0 %copy-start.2 = (bf16[128,1536]{1,0:T(8,128)(2,1)}, bf16[128,1536]{1,0:T(8,128)(2,1)S(1)}, u32[]{:S(2)}) copy-start(bf16[128,1536]{1,0:T(8,128)(2,1)S(1)} %add_convert_fusion) | copy-start | bytes 1179652
  98.8 27.6 %copy-start.9 = (f32[3,3,256]{2,1,0:T(4,128)S(1)}, f32[3,3,256]{2,1,0:T(4,128)}, u32[]{:S(2)}) copy-start(f32[3,3,256]{2,1,0:T(4,128)} %param.23) | copy-start | bytes 27652
  114.1 14.2 %copy-start.11 = (f32[256]{0:T(256)S(1)}, f32[256]{0:T(256)}, u32[]{:S(2)}) copy-start(f32[256]{0:T(256)} %param.24) | copy-start | bytes 3076
  114.2 14.2 %copy-start.3 = (bf16[256,1024]{1,0:T(8,128)(2,1)S(1)}, bf16[256,1024]{1,0:T(8,128)(2,1)}, u32[]{:S(2)}) copy-start(bf16[256,1024]{1,0:T(8,128)(2,1)} %param.25) | copy-start | bytes 1572868
  114.3 2.9 %collective-permute-start.7 = (bf16[1,32,256]{2,1,0:T(8,128)(2,1)S(1)}, bf16[1,32,256]{2,1,0:T(8,128)(2,1)S(1)}, u32[]{:S(2)}, u32[]{:S(2)}) collective-permute-start(bf16[1,32,256]{2,1,0:T(8,128)(2,1)S(1)} %get-tuple-element.7), channel_id=1, source_target_pairs={{0,4},{4,8},{8,12},{12,16},{16,20},{20,24},{24,28},{1,5},{5,9},{9,... | collective-permute-start | bytes 49160 | tf_op jit(solution)/shard_map/ppermute | solution.py:36
  115.7 4.8 %collective-permute-start.8 = (bf16[1,32,256]{2,1,0:T(8,128)(2,1)S(1)}, bf16[1,32,256]{2,1,0:T(8,128)(2,1)S(1)}, u32[]{:S(2)}, u32[]{:S(2)}) collective-permute-start(bf16[1,32,256]{2,1,0:T(8,128)(2,1)S(1)} %get-tuple-element.8), channel_id=1, source_target_pairs={{4,0},{8,4},{12,8},{16,12},{20,16},{24,20},{28,24},{5,1},{9,5},{13... | collective-permute-start | bytes 49160 | tf_op jit(solution)/shard_map/ppermute | solution.py:39
  120.5 5.9 %collective-permute-start.10 = (bf16[10,1,256]{2,1,0:T(2,128)(2,1)S(1)}, bf16[10,1,256]{2,1,0:T(2,128)(2,1)S(1)}, u32[]{:S(2)}, u32[]{:S(2)}) collective-permute-start(bf16[10,1,256]{2,1,0:T(2,128)(2,1)S(1)} %get-tuple-element.6), channel_id=1, source_target_pairs={{1,0},{2,1},{3,2},{5,4},{6,5},{7,6},{9,8},{10,9},{11,10},{13,12},{... | collective-permute-start | bytes 15368 | tf_op jit(solution)/shard_map/ppermute | solution.py:39
  121.8 5.9 %collective-permute-start.9 = (bf16[10,1,256]{2,1,0:T(2,128)(2,1)S(1)}, bf16[10,1,256]{2,1,0:T(2,128)(2,1)S(1)}, u32[]{:S(2)}, u32[]{:S(2)}) collective-permute-start(bf16[10,1,256]{2,1,0:T(2,128)(2,1)S(1)} %get-tuple-element.5), channel_id=1, source_target_pairs={{0,1},{1,2},{2,3},{4,5},{5,6},{6,7},{8,9},{9,10},{10,11},{12,13},{... | collective-permute-start | bytes 15368 | tf_op jit(solution)/shard_map/ppermute | solution.py:36
Sparse Core Ops, SparseCore 0:
  9.9 39.9 all-gather.1
  56.9 40.7 reduce-scatter.2
  135.3 140.8 reduce-scatter.4
